TPU v7x, 256 devices: a whole 4x4x8 slice. The times are simulated.
256 devices in a mesh: section: 8 (over y, core), chan: 32 (over z, x).
Axes of the slice: x: 4, y: 4, z: 8, core: 2. Of those that a mesh axis runs over, the one named last changes fastest.
Arguments:
- prompt: bfloat16 [192, 8192], P(None, 'chan'), may hold values from -6 to 6
- norm_gain: bfloat16 [8, 8192], P('section', 'chan'), may hold values from 0.5 to 1.5
- in_weight: bfloat16 [8, 8192, 3, 8192], P('section', None, None, 'chan'), may hold values from -0.0625 to 0.0625
- feat_taps: float32 [8, 3, 3, 8192], P('section', None, None, 'chan'), may hold values from -3 to 3
- fir_taps: float32 [8, 128, 512], P('section', None, 'chan'), may hold values from -0.5 to 0.5
- residues: float32 [8, 16, 512], P('section', None, 'chan'), may hold values from -0.2 to 0.2
- decay: float32 [8, 16, 512], P('section', None, 'chan'), may hold values from 0.002 to 0.1
Outputs:
- section_out: bfloat16 [8, 192, 8192], P('section', None, 'chan')
All inputs are finite; a program needn't handle non-finite values.
Results may differ from a plain program's by a relative error of at most 0.019.
Values may be sent and summed in bfloat16 or wider, within the bound.
A program may use at most 128 MiB of HBM per device.

v0:
```python
import jax
import jax.numpy as jnp
from jax import lax
from jax.sharding import PartitionSpec as P

BLOCK_TOK = 64
NBLOCKS = 3


EPSILON = 1e-06


def shifted(value, axis, steps):
    count = lax.axis_size(axis)
    initial, last = (max(0, -steps), min(count, count - steps))
    return lax.ppermute(value, axis, [(source, source + steps) for source in range(initial, last)])


def body(prompt, norm_gain, in_weight, feat_taps, fir_taps, residues, decay):
    block_len = BLOCK_TOK
    num_blocks = NBLOCKS
    width = in_weight.shape[1]
    local = prompt.shape[1]
    groups_local = fir_taps.shape[2]
    group_size = local // groups_local
    fir_len = fir_taps.shape[1]
    sections = lax.axis_size("section")
    section_idx = lax.axis_index("section")
    is_medium = section_idx % 2 == 0
    weight = in_weight[0].reshape(width, 3 * local)
    tap_rows = feat_taps[0]
    fir_section = fir_taps[0]
    residue_section = residues[0]
    rate_section = decay[0]
    out_pos = jnp.arange(block_len)
    in_pos = jnp.arange(fir_len + block_len)
    fir_lag = out_pos[:, None] + fir_len - in_pos[None, :]
    fir_ok = (fir_lag >= 0) & (fir_lag < fir_len)
    fir_table = jnp.where(fir_ok[None], fir_section.T[:, jnp.clip(fir_lag, 0, fir_len - 1)], 0.0)
    inner_lag = out_pos[:, None] - (in_pos[None, :] - fir_len)
    inner_ok = (inner_lag >= 0) & (in_pos[None, :] >= fir_len)
    lag_values = out_pos.astype(jnp.float32)
    powers = jnp.exp(-rate_section[None, :, :] * lag_values[:, None, None])
    modal = jnp.einsum("ng,jng->jg", residue_section, powers, precision=lax.Precision.HIGHEST)
    modal_table = jnp.where(inner_ok[None], modal.T[:, jnp.clip(inner_lag, 0, block_len - 1)], 0.0)
    toeplitz = jnp.where(is_medium, fir_table, modal_table)
    carry_coef = residue_section[None] * jnp.exp(
        -rate_section[None] * (lag_values + 1.0)[:, None, None]
    )
    carry_coef = jnp.where(is_medium, 0.0, carry_coef)
    feed_coef = jnp.exp(-rate_section[None] * (block_len - 1.0 - lag_values)[:, None, None])
    block_decay = jnp.exp(-rate_section * block_len)

    def add_rows(shard_piece):
        return jnp.dot(shard_piece, weight, preferred_element_type=jnp.float32)

    def turn(carried, turn_index):
        incoming, proj_cache, kv_cache, modal_state, out_buffer = carried
        which = turn_index - section_idx
        is_live = (which >= 0) & (which < num_blocks)
        begin_row = jnp.clip(which, 0, num_blocks - 1) * block_len
        first_rows = lax.dynamic_slice_in_dim(prompt, begin_row, block_len, 0)
        rows_in = jnp.where(section_idx == 0, first_rows, incoming)
        inputs_f = rows_in.astype(jnp.float32)
        partial_sq = jnp.sum(inputs_f * inputs_f, axis=1)
        squares = lax.psum(partial_sq, "chan")
        normed = (
            inputs_f * lax.rsqrt(squares[:, None] / width + EPSILON) * norm_gain.astype(jnp.float32)
        ).astype(jnp.bfloat16)
        projected = add_rows(lax.all_gather(normed, "chan", axis=1, tiled=True))
        projected = projected.reshape(block_len, 3, local)
        extended = jnp.concatenate([proj_cache, projected], axis=0)
        features = (
            tap_rows[0] * extended[2:] + tap_rows[1] * extended[1:-1] + tap_rows[2] * extended[:-2]
        )
        product_kv = features[:, 1] * features[:, 2]
        window = jnp.concatenate([kv_cache, product_kv], axis=0)
        grouped = window.reshape(fir_len + block_len, groups_local, group_size)
        convolved = jnp.einsum("gts,sgk->tgk", toeplitz, grouped, precision=lax.Precision.HIGHEST)
        convolved = convolved + jnp.einsum(
            "tng,ngk->tgk", carry_coef, modal_state, precision=lax.Precision.HIGHEST
        )
        new_state = block_decay[:, :, None] * modal_state + jnp.einsum(
            "tng,tgk->ngk", feed_coef, grouped[fir_len:], precision=lax.Precision.HIGHEST
        )
        result = (inputs_f + features[:, 0] * convolved.reshape(block_len, local)).astype(
            jnp.bfloat16
        )
        proj_cache = jnp.where(is_live, extended[block_len:], proj_cache)
        kv_cache = jnp.where(is_live, window[block_len:], kv_cache)
        modal_state = jnp.where(is_live, new_state, modal_state)
        out_buffer = jnp.where(
            is_live, lax.dynamic_update_slice_in_dim(out_buffer, result, begin_row, 0), out_buffer
        )
        passed = shifted(result, "section", 1)
        return ((passed, proj_cache, kv_cache, modal_state, out_buffer), None)

    initial = (
        jnp.zeros((block_len, local), jnp.bfloat16),
        jnp.zeros((2, 3, local), jnp.float32),
        jnp.zeros((fir_len, local), jnp.float32),
        jnp.zeros((residues.shape[1], groups_local, group_size), jnp.float32),
        jnp.zeros((block_len * num_blocks, local), jnp.bfloat16),
    )
    finals, unused = lax.scan(turn, initial, jnp.arange(num_blocks + sections - 1, dtype=jnp.int32))
    return finals[4][None]


def solution(mesh):
    return jax.shard_map(
        body,
        mesh=mesh,
        in_specs=(
            P(None, "chan"),
            P("section", "chan"),
            P("section", None, None, "chan"),
            P("section", None, None, "chan"),
            P("section", None, "chan"),
            P("section", None, "chan"),
            P("section", None, "chan"),
        ),
        out_specs=P("section", None, "chan"),
        check_vma=False,
    )
```

profile of v0, /device:TPU:25, one launch (start us, length us, event | category | flops | bytes accessed | tf_op | source)
XLA Modules:
  0.0 1728.1 jit_solution(16256413265977966794)
XLA Ops:
  7.2 16.7 copy.26
  23.9 16.7 copy.33
  41.1 41.1 %gather_fusion.1 = f32[12288,16]{1,0:T(8,128)} fusion(f32[16,64]{0,1:T(8,128)S(1)} %multiply_reduce_fusion, s32[12288]{0:T(1024)S(1)} %broadcast_clamp_fusion), kind=kCustom, calls=%fused_computation.1 | custom fusion | bytes 1622016 | tf_op jit(solution)/shard_map/gather | solution.py:45
  87.5 41.1 %gather_fusion = f32[12288,16]{1,0:T(8,128)} fusion(f32[16,128]{0,1:T(8,128)S(1)} %bitcast.82, s32[12288]{0:T(1024)S(1)} %broadcast_clamp_fusion.1), kind=kCustom, calls=%fused_computation | custom fusion | bytes 1622016 | tf_op jit(solution)/shard_map/gather | solution.py:39
  133.9 1586.7 %while.22 = (s32[]{:T(128)}, bf16[64,256]{1,0:T(8,128)(2,1)S(1)}, f32[2,3,256]{2,1,0:T(4,128)S(1)}, f32[128,256]{0,1:T(8,128)S(1)}, f32[16,16,16]{0,2,1:T(8,128)...) while((s32[]{:T(128)}, bf16[64,256]{1,0:T(8,128)(2,1)S(1)}, ...), condition=%wide.region_3.4_spmd.clone.clone.clone, body=%wide.region_0.3_spmd.clone.clone.clone.sunk | while | flops 850173312 | bytes 21374916 | solution.py:105
  136.1 63.5 %psum.12 = f32[64]{0:T(128)S(1)} all-reduce(f32[64]{0:T(128)S(1)} %get-tuple-element.554), channel_id=1, replica_groups=mesh['section'=8,'chan'=32] {'chan'}, use_global_device_ids=true, to_apply=%region_2.2 | all-reduce | flops 64 | bytes 512 | tf_op jit(solution)/shard_map/while/body/eval_jaxpr/psum | solution.py:66
  200.4 75.8 %all-gather.2.cloned.1.call-done = bf16[64,8192]{1,0:T(8,128)(2,1)} async-done(((bf16[64,256]{1,0:T(8,128)(2,1)}), bf16[64,8192]{1,0:T(8,128)(2,1)}) %all-gather.2.cloned.1.call-update) | async-done | bytes 1048592 | tf_op jit(solution)/shard_map/while/body/eval_jaxpr/all_gather | solution.py:70
  276.1 7.2 fusion.73
  294.8 60.0 %psum.12 = f32[64]{0:T(128)S(1)} all-reduce(f32[64]{0:T(128)S(1)} %get-tuple-element.554), channel_id=1, replica_groups=mesh['section'=8,'chan'=32] {'chan'}, use_global_device_ids=true, to_apply=%region_2.2 | all-reduce | flops 64 | bytes 512 | tf_op jit(solution)/shard_map/while/body/eval_jaxpr/psum | solution.py:66
  355.6 79.3 %all-gather.2.cloned.1.call-done = bf16[64,8192]{1,0:T(8,128)(2,1)} async-done(((bf16[64,256]{1,0:T(8,128)(2,1)}), bf16[64,8192]{1,0:T(8,128)(2,1)}) %all-gather.2.cloned.1.call-update) | async-done | bytes 1048592 | tf_op jit(solution)/shard_map/while/body/eval_jaxpr/all_gather | solution.py:70
  434.8 7.2 fusion.73
  453.4 60.0 %psum.12 = f32[64]{0:T(128)S(1)} all-reduce(f32[64]{0:T(128)S(1)} %get-tuple-element.554), channel_id=1, replica_groups=mesh['section'=8,'chan'=32] {'chan'}, use_global_device_ids=true, to_apply=%region_2.2 | all-reduce | flops 64 | bytes 512 | tf_op jit(solution)/shard_map/while/body/eval_jaxpr/psum | solution.py:66
  514.2 79.3 %all-gather.2.cloned.1.call-done = bf16[64,8192]{1,0:T(8,128)(2,1)} async-done(((bf16[64,256]{1,0:T(8,128)(2,1)}), bf16[64,8192]{1,0:T(8,128)(2,1)}) %all-gather.2.cloned.1.call-update) | async-done | bytes 1048592 | tf_op jit(solution)/shard_map/while/body/eval_jaxpr/all_gather | solution.py:70
  593.5 7.2 fusion.73
  612.1 60.0 %psum.12 = f32[64]{0:T(128)S(1)} all-reduce(f32[64]{0:T(128)S(1)} %get-tuple-element.554), channel_id=1, replica_groups=mesh['section'=8,'chan'=32] {'chan'}, use_global_device_ids=true, to_apply=%region_2.2 | all-reduce | flops 64 | bytes 512 | tf_op jit(solution)/shard_map/while/body/eval_jaxpr/psum | solution.py:66
  672.9 79.2 %all-gather.2.cloned.1.call-done = bf16[64,8192]{1,0:T(8,128)(2,1)} async-done(((bf16[64,256]{1,0:T(8,128)(2,1)}), bf16[64,8192]{1,0:T(8,128)(2,1)}) %all-gather.2.cloned.1.call-update) | async-done | bytes 1048592 | tf_op jit(solution)/shard_map/while/body/eval_jaxpr/all_gather | solution.py:70
  752.1 7.2 fusion.73
  770.8 60.0 %psum.12 = f32[64]{0:T(128)S(1)} all-reduce(f32[64]{0:T(128)S(1)} %get-tuple-element.554), channel_id=1, replica_groups=mesh['section'=8,'chan'=32] {'chan'}, use_global_device_ids=true, to_apply=%region_2.2 | all-reduce | flops 64 | bytes 512 | tf_op jit(solution)/shard_map/while/body/eval_jaxpr/psum | solution.py:66
  831.6 79.3 %all-gather.2.cloned.1.call-done = bf16[64,8192]{1,0:T(8,128)(2,1)} async-done(((bf16[64,256]{1,0:T(8,128)(2,1)}), bf16[64,8192]{1,0:T(8,128)(2,1)}) %all-gather.2.cloned.1.call-update) | async-done | bytes 1048592 | tf_op jit(solution)/shard_map/while/body/eval_jaxpr/all_gather | solution.py:70
  929.4 60.0 %psum.12 = f32[64]{0:T(128)S(1)} all-reduce(f32[64]{0:T(128)S(1)} %get-tuple-element.554), channel_id=1, replica_groups=mesh['section'=8,'chan'=32] {'chan'}, use_global_device_ids=true, to_apply=%region_2.2 | all-reduce | flops 64 | bytes 512 | tf_op jit(solution)/shard_map/while/body/eval_jaxpr/psum | solution.py:66
  990.2 79.2 %all-gather.2.cloned.1.call-done = bf16[64,8192]{1,0:T(8,128)(2,1)} async-done(((bf16[64,256]{1,0:T(8,128)(2,1)}), bf16[64,8192]{1,0:T(8,128)(2,1)}) %all-gather.2.cloned.1.call-update) | async-done | bytes 1048592 | tf_op jit(solution)/shard_map/while/body/eval_jaxpr/all_gather | solution.py:70
  1069.5 7.2 fusion.73
  1088.1 60.0 %psum.12 = f32[64]{0:T(128)S(1)} all-reduce(f32[64]{0:T(128)S(1)} %get-tuple-element.554), channel_id=1, replica_groups=mesh['section'=8,'chan'=32] {'chan'}, use_global_device_ids=true, to_apply=%region_2.2 | all-reduce | flops 64 | bytes 512 | tf_op jit(solution)/shard_map/while/body/eval_jaxpr/psum | solution.py:66
  1148.9 79.3 %all-gather.2.cloned.1.call-done = bf16[64,8192]{1,0:T(8,128)(2,1)} async-done(((bf16[64,256]{1,0:T(8,128)(2,1)}), bf16[64,8192]{1,0:T(8,128)(2,1)}) %all-gather.2.cloned.1.call-update) | async-done | bytes 1048592 | tf_op jit(solution)/shard_map/while/body/eval_jaxpr/all_gather | solution.py:70
  1246.8 60.0 %psum.12 = f32[64]{0:T(128)S(1)} all-reduce(f32[64]{0:T(128)S(1)} %get-tuple-element.554), channel_id=1, replica_groups=mesh['section'=8,'chan'=32] {'chan'}, use_global_device_ids=true, to_apply=%region_2.2 | all-reduce | flops 64 | bytes 512 | tf_op jit(solution)/shard_map/while/body/eval_jaxpr/psum | solution.py:66
  1307.6 79.2 %all-gather.2.cloned.1.call-done = bf16[64,8192]{1,0:T(8,128)(2,1)} async-done(((bf16[64,256]{1,0:T(8,128)(2,1)}), bf16[64,8192]{1,0:T(8,128)(2,1)}) %all-gather.2.cloned.1.call-update) | async-done | bytes 1048592 | tf_op jit(solution)/shard_map/while/body/eval_jaxpr/all_gather | solution.py:70
  1386.8 7.2 fusion.73
  1405.4 60.0 %psum.12 = f32[64]{0:T(128)S(1)} all-reduce(f32[64]{0:T(128)S(1)} %get-tuple-element.554), channel_id=1, replica_groups=mesh['section'=8,'chan'=32] {'chan'}, use_global_device_ids=true, to_apply=%region_2.2 | all-reduce | flops 64 | bytes 512 | tf_op jit(solution)/shard_map/while/body/eval_jaxpr/psum | solution.py:66
  1466.2 79.3 %all-gather.2.cloned.1.call-done = bf16[64,8192]{1,0:T(8,128)(2,1)} async-done(((bf16[64,256]{1,0:T(8,128)(2,1)}), bf16[64,8192]{1,0:T(8,128)(2,1)}) %all-gather.2.cloned.1.call-update) | async-done | bytes 1048592 | tf_op jit(solution)/shard_map/while/body/eval_jaxpr/all_gather | solution.py:70
  1564.1 60.0 %psum.12 = f32[64]{0:T(128)S(1)} all-reduce(f32[64]{0:T(128)S(1)} %get-tuple-element.554), channel_id=1, replica_groups=mesh['section'=8,'chan'=32] {'chan'}, use_global_device_ids=true, to_apply=%region_2.2 | all-reduce | flops 64 | bytes 512 | tf_op jit(solution)/shard_map/while/body/eval_jaxpr/psum | solution.py:66
  1624.9 79.2 %all-gather.2.cloned.1.call-done = bf16[64,8192]{1,0:T(8,128)(2,1)} async-done(((bf16[64,256]{1,0:T(8,128)(2,1)}), bf16[64,8192]{1,0:T(8,128)(2,1)}) %all-gather.2.cloned.1.call-update) | async-done | bytes 1048592 | tf_op jit(solution)/shard_map/while/body/eval_jaxpr/all_gather | solution.py:70
  1704.1 7.2 fusion.73
  (291 shorter events, 148.0 us)
Async XLA Ops:
  23.9 16.7 copy-start.4
  23.9 16.8 copy-start.1
  40.6 46.6 %copy-start.3 = (f32[1,128,16]{1,2,0:T(8,128)S(1)}, f32[1,128,16]{1,2,0:T(8,128)}, u32[]{:S(2)}) copy-start(f32[1,128,16]{1,2,0:T(8,128)} %param.13) | copy-start | bytes 24580
  82.3 51.6 %copy-start.2 = (bf16[1,256]{1,0:T(2,128)(2,1)S(1)}, bf16[1,256]{1,0:T(2,128)(2,1)}, u32[]{:S(2)}) copy-start(bf16[1,256]{1,0:T(2,128)(2,1)} %param.10) | copy-start | bytes 1540
  133.9 142.2 %all-gather.2.cloned.1.call-start = ((), (), s32[]{:S(2)}) async-start(), calls=%async_computation | async-start | bytes 1081344 | tf_op jit(solution)/shard_map/while/body/eval_jaxpr/all_gather | solution.py:70
  285.3 7.3 collective-permute-start
  292.6 142.2 %all-gather.2.cloned.1.call-start = ((), (), s32[]{:S(2)}) async-start(), calls=%async_computation | async-start | bytes 1081344 | tf_op jit(solution)/shard_map/while/body/eval_jaxpr/all_gather | solution.py:70
  443.9 7.3 collective-permute-start
  451.3 142.2 %all-gather.2.cloned.1.call-start = ((), (), s32[]{:S(2)}) async-start(), calls=%async_computation | async-start | bytes 1081344 | tf_op jit(solution)/shard_map/while/body/eval_jaxpr/all_gather | solution.py:70
  602.6 7.3 collective-permute-start
  610.0 142.2 %all-gather.2.cloned.1.call-start = ((), (), s32[]{:S(2)}) async-start(), calls=%async_computation | async-start | bytes 1081344 | tf_op jit(solution)/shard_map/while/body/eval_jaxpr/all_gather | solution.py:70
  761.3 7.3 collective-permute-start
  768.6 142.2 %all-gather.2.cloned.1.call-start = ((), (), s32[]{:S(2)}) async-start(), calls=%async_computation | async-start | bytes 1081344 | tf_op jit(solution)/shard_map/while/body/eval_jaxpr/all_gather | solution.py:70
  919.9 7.3 collective-permute-start
  927.3 142.2 %all-gather.2.cloned.1.call-start = ((), (), s32[]{:S(2)}) async-start(), calls=%async_computation | async-start | bytes 1081344 | tf_op jit(solution)/shard_map/while/body/eval_jaxpr/all_gather | solution.py:70
  1078.6 7.3 collective-permute-start
  1085.9 142.2 %all-gather.2.cloned.1.call-start = ((), (), s32[]{:S(2)}) async-start(), calls=%async_computation | async-start | bytes 1081344 | tf_op jit(solution)/shard_map/while/body/eval_jaxpr/all_gather | solution.py:70
  1237.3 7.3 collective-permute-start
  1244.6 142.2 %all-gather.2.cloned.1.call-start = ((), (), s32[]{:S(2)}) async-start(), calls=%async_computation | async-start | bytes 1081344 | tf_op jit(solution)/shard_map/while/body/eval_jaxpr/all_gather | solution.py:70
  1395.9 7.3 collective-permute-start
  1403.3 142.2 %all-gather.2.cloned.1.call-start = ((), (), s32[]{:S(2)}) async-start(), calls=%async_computation | async-start | bytes 1081344 | tf_op jit(solution)/shard_map/while/body/eval_jaxpr/all_gather | solution.py:70
  1554.6 7.3 collective-permute-start
  1561.9 142.2 %all-gather.2.cloned.1.call-start = ((), (), s32[]{:S(2)}) async-start(), calls=%async_computation | async-start | bytes 1081344 | tf_op jit(solution)/shard_map/while/body/eval_jaxpr/all_gather | solution.py:70
  1713.3 7.3 collective-permute-start
  1720.6 0.6 copy-start
Sparse Core Ops, SparseCore 0:
  200.4 75.6 all-gather.1
  355.6 79.1 all-gather.1
  514.3 79.1 all-gather.1
  673.0 79.1 all-gather.1
  831.6 79.1 all-gather.1
  990.3 79.1 all-gather.1
  1149.0 79.1 all-gather.1
  1307.6 79.1 all-gather.1
  1466.3 79.1 all-gather.1
  1625.0 79.1 all-gather.1
where the time goes:
time: 1730 us
  waiting for transfers between devices  844 us (49%)
  blocking collectives  604 us (35%)
  local copies, waits for them, and re-layouts  136 us (8%)
  matrix products  88.7 us (5%)
  other arithmetic  20.9 us (1%)
    all_gather x10, waiting for transfers between devices, turn(): projected = add_rows(lax.all_gather(normed, 'chan', axis=1, tiled=True))  789 us
    psum x10, blocking collectives, turn(): squares = lax.psum(partial_sq, 'chan')  604 us
    dot_general x10, matrix products, add_rows(): return jnp.dot(shard_piece, weight, preferred_element_type=jnp.float32)  71.6 us
    ppermute x10, waiting for transfers between devices, shifted(): lax.ppermute(value, axis, [(source, source + steps) for source in range(i...  54.8 us
    gather x2, local copies, waits for them, and re-layouts, body(): modal.T[:, jnp.clip(inner_lag, 0, block_len - 1)]  46 us
    gather x2, local copies, waits for them, and re-layouts, body(): fir_section.T[:, jnp.clip(fir_lag, 0, fir_len - 1)]  46 us
    unnamed x16, local copies, waits for them, and re-layouts  34.9 us
  transfers between devices with their start and end apart: 20, of which 20 were waited for; matrix products, arithmetic and copies ran while one was open for 0% of the time, Pallas kernels for 0%

commit v1 on v0

v1 whole, which is shorter than its diff:
```python
import functools

import jax
import jax.numpy as jnp
from jax import lax
from jax.experimental import pallas as pl
from jax.experimental.pallas import tpu as pltpu
from jax.sharding import PartitionSpec as P

MESH = pl.DeviceIdType.MESH
EPSILON = 1e-06
BLOCK = 32
XS = 4
DIRECT_FROM = 8


def ring_offsets(zs):
    offs = [0]
    for d in range(1, zs // 2 + 1):
        offs.append(d)
        if zs - d != d:
            offs.append(zs - d)
    return offs


def kernel(
    dims,
    prompt_ref, gain_ref, w_hbm, taps_ref, fir_ref, res_ref, decay_ref,
    o_ref,
    wbuf, xbuf, gbuf, gown, pbuf, fpad, gpad, tbuf, rhs,
    wsem, zsem, xsem, gsem, ssem,
):
    secs, zs, length = dims
    rows = BLOCK
    nblk = length // rows
    width = zs * XS * 256
    offs = ring_offsets(zs)
    fwd = [k for k in range(zs) if k < DIRECT_FROM]
    direct = [k for k in range(zs) if k >= DIRECT_FROM]
    sec = lax.axis_index("section")
    chan = lax.axis_index("chan")
    z = chan // XS
    x = lax.rem(chan, XS)

    def z_at(delta):
        return lax.rem(z + delta + 2 * zs, zs)

    def x_at(delta):
        return lax.rem(x + delta + 2 * XS, XS)

    def dev(s, zi, xi):
        return (s, zi * XS + xi)

    def w_copy(xr, k):
        chunk = z_at(offs[k]) * XS + x_at(xr)
        start = pl.multiple_of(chunk * 256, 256)
        return pltpu.make_async_copy(
            w_hbm.at[:, pl.ds(start, 256), :],
            wbuf.at[:, xr, pl.ds(k * 256, 256), :],
            wsem.at[xr],
        )

    for xr in range(XS):
        for k in range(zs):
            w_copy(xr, k).start()

    gown[...] = gain_ref[...].astype(jnp.float32)

    barrier = pltpu.get_barrier_semaphore()

    def hello(s, zi, xi):
        pl.semaphore_signal(barrier, inc=1, device_id=dev(s, zi, xi), device_id_type=MESH)

    for k in range(1, zs):
        hello(sec, z_at(offs[k]), x)
    for xr in range(1, XS):
        hello(sec, z, x_at(xr))

    @pl.when(sec == 0)
    def _():
        for k in direct:
            for xr in range(1, XS):
                hello(sec, z_at(offs[k]), x_at(xr))

    @pl.when(sec > 0)
    def _():
        for k in range(zs):
            hello(sec - 1, z_at(offs[k]), x)
        for k in direct:
            for xr in range(1, XS):
                hello(sec - 1, z_at(offs[k]), x_at(xr))

    greetings = zs - 1 + XS - 1
    greetings = greetings + jnp.where(sec == 0, len(direct) * (XS - 1), 0)
    greetings = greetings + jnp.where(sec < secs - 1, zs + len(direct) * (XS - 1), 0)
    pl.semaphore_wait(barrier, greetings)

    def send_block(src, target, b, own):
        for k in reversed(range(zs)):
            for xr in range(XS) if k in direct else (0,):
                sem = zsem.at[b, k] if xr == 0 else xsem.at[b, xr - 1]
                dst = xbuf.at[b, xr, k]
                if own and k == 0 and xr == 0:
                    pltpu.make_async_copy(src, dst, sem).start()
                else:
                    pltpu.make_async_remote_copy(
                        src_ref=src, dst_ref=dst,
                        send_sem=ssem.at[0 if xr == 0 else 1], recv_sem=sem,
                        device_id=dev(target, z_at(-offs[k]), x_at(-xr)), device_id_type=MESH,
                    ).start()

    @pl.when(sec == 0)
    def _():
        send_block(prompt_ref.at[pl.ds(0, rows), :], 0, 0, True)

    pltpu.make_async_copy(gown, gbuf.at[0, 0], gsem.at[0]).start()
    for k in range(1, zs):
        pltpu.make_async_remote_copy(
            src_ref=gown, dst_ref=gbuf.at[0, k], send_sem=ssem.at[3], recv_sem=gsem.at[0],
            device_id=dev(sec, z_at(-offs[k]), x), device_id_type=MESH,
        ).start()

    @pl.when(sec == 0)
    def _():
        @pl.loop(1, nblk)
        def _(b):
            start = pl.multiple_of(b * rows, rows)
            send_block(prompt_ref.at[pl.ds(start, rows), :], 0, b, True)

    pad = rows
    fpad[...] = jnp.zeros_like(fpad)
    medium = lax.rem(sec, 2) == 0

    @pl.when(medium)
    def _():
        spread = (
            lax.broadcasted_iota(jnp.int32, (16, 128), 0)
            == lax.rem(lax.broadcasted_iota(jnp.int32, (16, 128), 1), 16)
        ).astype(jnp.float32)
        taps = lax.dot_general(
            fir_ref[...], spread, (((0,), (0,)), ((), ())),
            precision=lax.Precision.HIGHEST, preferred_element_type=jnp.float32,
        )
        count = min(fir_ref.shape[1], length)
        fpad[pl.ds(pad, count), :] = taps[:count]

    @pl.when(jnp.logical_not(medium))
    def _():
        lags = lax.broadcasted_iota(jnp.int32, (length, 128), 0).astype(jnp.float32)
        res = jnp.concatenate([res_ref[...]] * 8, axis=1)
        rate = jnp.concatenate([decay_ref[...]] * 8, axis=1)
        total = jnp.zeros((length, 128), jnp.float32)
        for n in range(res.shape[0]):
            total = total + res[n : n + 1] * jnp.exp(-rate[n : n + 1] * lags)
        fpad[pl.ds(pad, length), :] = total

    span = length + rows - 8
    lane_row = lax.broadcasted_iota(jnp.int32, (1, 128), 1) // 16
    shifted = jnp.zeros((span, 128), jnp.float32)
    for i in range(8):
        shifted = jnp.where(lane_row == i, fpad[pl.ds(8 - i, span), :], shifted)
    gpad[...] = shifted
    for d in range(nblk):
        for q in range(rows // 8):
            lo = d * rows - 8 * q + rows - 8
            tbuf[d, :, pl.ds(q * 128, 128)] = gpad[pl.ds(lo, rows), :].astype(jnp.bfloat16)

    pbuf[...] = jnp.zeros_like(pbuf)

    pltpu.make_async_copy(gbuf.at[0], gbuf.at[0], gsem.at[0]).wait()
    for xr in range(1, XS):
        pltpu.make_async_remote_copy(
            src_ref=gbuf.at[0], dst_ref=gbuf.at[xr], send_sem=ssem.at[4], recv_sem=gsem.at[xr],
            device_id=dev(sec, z, x_at(-xr)), device_id_type=MESH,
        ).start()

    def forward(b):
        for k in fwd:
            pltpu.make_async_copy(xbuf.at[b, 0, k], xbuf.at[b, 0, k], zsem.at[b, k]).wait()
            for xr in (2, 1, 3):
                pltpu.make_async_remote_copy(
                    src_ref=xbuf.at[b, 0, k], dst_ref=xbuf.at[b, xr, k],
                    send_sem=ssem.at[2], recv_sem=xsem.at[b, xr - 1],
                    device_id=dev(sec, z, x_at(-xr)), device_id_type=MESH,
                ).start()

    def product(b, xr, acc, squares):
        pieces = []
        for k in range(zs):
            piece = xbuf[b, xr, k].astype(jnp.float32)
            square = piece * piece
            squares = squares + (square[:, :128] + square[:, 128:])
            pieces.append((piece * gbuf[xr, k]).astype(jnp.bfloat16))
        left = jnp.concatenate(pieces, axis=1)
        return (
            tuple(
                acc[i] + jnp.dot(left, wbuf[i, xr], preferred_element_type=jnp.float32)
                for i in range(3)
            ),
            squares,
        )

    lane_group = lax.broadcasted_iota(jnp.int32, (16, 256), 1) // 16
    own_group = lane_group == lax.broadcasted_iota(jnp.int32, (16, 256), 0)

    forward(0)
    for xr in range(XS):
        pltpu.make_async_copy(wbuf.at[:, xr], wbuf.at[:, xr], wsem.at[xr]).wait()
    for xr in range(1, XS):
        pltpu.make_async_copy(gbuf.at[xr], gbuf.at[xr], gsem.at[xr]).wait()

    def block(b, carry):
        def earlier(d, total):
            return total + jnp.dot(tbuf[d], rhs[b - d], preferred_element_type=jnp.float32)

        conv = lax.fori_loop(1, b + 1, earlier, jnp.zeros((rows, 256), jnp.float32))
        for k in direct:
            pltpu.make_async_copy(xbuf.at[b, 0, k], xbuf.at[b, 0, k], zsem.at[b, k]).wait()
        acc = tuple(jnp.zeros((rows, 256), jnp.float32) for i in range(3))
        acc, squares = product(b, 0, acc, jnp.zeros((rows, 128), jnp.float32))

        def side(xr, state):
            pltpu.make_async_copy(xbuf.at[b, xr], xbuf.at[b, xr], xsem.at[b, xr - 1]).wait()
            return product(b, xr, *state)

        acc, squares = lax.fori_loop(1, XS, side, (acc, squares))
        scale = lax.rsqrt(jnp.sum(squares, axis=1, keepdims=True) / width + EPSILON)
        feats = []
        for i in range(3):
            pbuf[i, pl.ds(8, rows), :] = acc[i] * scale
            feats.append(
                taps_ref[i] * pbuf[i, pl.ds(8, rows), :]
                + taps_ref[3 + i] * pbuf[i, pl.ds(7, rows), :]
                + taps_ref[6 + i] * pbuf[i, pl.ds(6, rows), :]
            )
        kv = feats[1] * feats[2]
        for p in range(rows):
            rhs[b, pl.ds(p * 16, 16), :] = jnp.where(
                own_group, jnp.broadcast_to(kv[p : p + 1], (16, 256)), 0.0
            ).astype(jnp.bfloat16)
        conv = conv + jnp.dot(tbuf[0], rhs[b], preferred_element_type=jnp.float32)
        start = pl.multiple_of(b * rows, rows)
        result = xbuf[b, 0, 0].astype(jnp.float32) + feats[0] * conv
        o_ref[pl.ds(start, rows), :] = result.astype(jnp.bfloat16)

        @pl.when(sec < secs - 1)
        def _():
            send_block(o_ref.at[pl.ds(start, rows), :], sec + 1, b, False)

        for i in range(3):
            pbuf[i, pl.ds(0, 8), :] = pbuf[i, pl.ds(rows, 8), :]

        @pl.when(b < nblk - 1)
        def _():
            forward(b + 1)

        return carry

    lax.fori_loop(0, nblk, block, 0)

    def sent(view, which):
        pltpu.make_async_copy(view, view, ssem.at[which]).wait()

    @pl.when(sec == 0)
    def _():
        sent(xbuf.at[:, 0, pl.ds(1, zs - 1)], 0)
        if direct:
            sent(xbuf.at[:, pl.ds(1, XS - 1), pl.ds(0, len(direct))], 1)

    @pl.when(sec < secs - 1)
    def _():
        sent(xbuf.at[:, 0], 0)
        if direct:
            sent(xbuf.at[:, pl.ds(1, XS - 1), pl.ds(0, len(direct))], 1)

    if fwd:
        sent(xbuf.at[:, pl.ds(1, XS - 1), pl.ds(0, len(fwd))], 2)
    sent(gbuf.at[0, pl.ds(1, zs - 1)], 3)
    sent(gbuf.at[pl.ds(1, XS - 1)], 4)


def solution(mesh):
    secs = mesh.shape["section"]
    zs = mesh.shape["chan"] // XS

    def body(prompt, norm_gain, in_weight, feat_taps, fir_taps, residues, decay):
        length, local = prompt.shape
        rows = BLOCK
        nblk = length // rows
        vmem = pl.BlockSpec(memory_space=pltpu.VMEM)
        out = pl.pallas_call(
            functools.partial(kernel, (secs, zs, length)),
            name="relay",
            out_shape=jax.ShapeDtypeStruct((length, local), jnp.bfloat16),
            in_specs=[vmem, vmem, pl.BlockSpec(memory_space=pl.ANY), vmem, vmem, vmem, vmem],
            out_specs=vmem,
            scratch_shapes=[
                pltpu.VMEM((3, XS, zs * 256, 256), jnp.bfloat16),
                pltpu.VMEM((nblk, XS, zs, rows, 256), jnp.bfloat16),
                pltpu.VMEM((XS, zs, 1, 256), jnp.float32),
                pltpu.VMEM((1, 256), jnp.float32),
                pltpu.VMEM((3, 8 + rows, 256), jnp.float32),
                pltpu.VMEM((rows + length, 128), jnp.float32),
                pltpu.VMEM((rows + length - 8, 128), jnp.float32),
                pltpu.VMEM((nblk, rows, rows * 16), jnp.bfloat16),
                pltpu.VMEM((nblk, rows * 16, 256), jnp.bfloat16),
                pltpu.SemaphoreType.DMA((XS,)),
                pltpu.SemaphoreType.DMA((nblk, zs)),
                pltpu.SemaphoreType.DMA((nblk, XS - 1)),
                pltpu.SemaphoreType.DMA((XS,)),
                pltpu.SemaphoreType.DMA((5,)),
            ],
            compiler_params=pltpu.CompilerParams(
                collective_id=0, has_side_effects=True, vmem_limit_bytes=56 << 20
            ),
        )(
            prompt,
            norm_gain,
            in_weight[0].transpose(1, 0, 2),
            feat_taps[0].reshape(9, 1, local),
            fir_taps[0].T,
            residues[0],
            decay[0],
        )
        return out[None]

    return jax.shard_map(
        body,
        mesh=mesh,
        in_specs=(
            P(None, "chan"),
            P("section", "chan"),
            P("section", None, None, "chan"),
            P("section", None, None, "chan"),
            P("section", None, "chan"),
            P("section", None, "chan"),
            P("section", None, "chan"),
        ),
        out_specs=P("section", None, "chan"),
        check_vma=False,
    )
```

time: 1730 us -> 156 us (0.09)
  waiting for transfers between devices: 844 us -> 0 us
  blocking collectives: 604 us -> 0 us
  Pallas kernels: 0 us -> 154 us
  local copies, waits for them, and re-layouts: 136 us -> 1.54 us
  matrix products: 88.7 us -> 0 us
  other arithmetic: 20.9 us -> 0 us
    all_gather x10 -> x0, waiting for transfers between devices: 789 us -> none  [turn(): projected = add_rows(lax.all_gather(normed, 'chan', axis=1, tiled=True))]
    psum x10 -> x0, blocking collectives: 604 us -> none  [turn(): squares = lax.psum(partial_sq, 'chan')]
    pallas_call x0 -> x1, Pallas kernels: none -> 154 us  [body(): pl.pallas_call(functools.partial(kernel, (secs, zs, length)), name='relay...]
    gather x4 -> x0, local copies, waits for them, and re-layouts: 92 us -> none  [the longest x2 46 us: body(): modal.T[:, jnp.clip(inner_lag, 0, block_len - 1)]]
    dot_general x40 -> x0, matrix products: 88.7 us -> none  [the longest x10 71.6 us: add_rows(): return jnp.dot(shard_piece, weight, preferred_element_type=jnp.float32)]
    ppermute x10 -> x0, waiting for transfers between devices: 54.8 us -> none  [shifted(): lax.ppermute(value, axis, [(source, source + steps) for source in range(i...]
    unnamed x16 -> x1, local copies, waits for them, and re-layouts: 34.9 us -> 1.54 us
  transfers between devices with their start and end apart: 20 -> 0, of which waited for: 20 -> 0; matrix products, arithmetic and copies ran while one was open for 0% -> 0% of each run, Pallas kernels for 0% -> 0%
where the time goes in v1:
time: 156 us
  Pallas kernels  154 us (99%)
    pallas_call x1, Pallas kernels, body(): pl.pallas_call(functools.partial(kernel, (secs, zs, length)), name='relay...  154 us

profile of v1, /device:TPU:25, one launch (start us, length us, event | category | flops | bytes accessed | tf_op | source)
XLA Modules:
  0.0 155.6 jit_solution(18187356712750444706)
XLA Ops:
  0.0 154.1 %relay.1 = bf16[192,256]{1,0:T(8,128)(2,1)} custom-call(bf16[192,256]{1,0:T(8,128)(2,1)} %prompt_ref.1, bf16[1,256]{1,0:T(2,128)(2,1)} %gain_ref.1, bf16[3,8192,256]{2,1,0:T(8,128)(2,1)} %bitcast.10, f32[9,1,256]{2,1,0:T(1,128)} %bitcast.12, f32[16,128]{1,0:T(8,128)} %bitcast.13, f32[16,16]{1,0:T(8,128)} %bitcast.14, f32[16,16]{1,0:T(8,128)} %bitcast.15), custom_call_target="tpu_custom_call" | custom-call | tf_op jit(solution)/shard_map/relay/pallas_call | solution.py:291
  154.1 1.5 copy.9

commit v2 on v1

--- a/solution.py
+++ b/solution.py
@@ -9,9 +9,14 @@
 
 MESH = pl.DeviceIdType.MESH
 EPSILON = 1e-06
-BLOCK = 32
+BLOCK = 16
 XS = 4
 DIRECT_FROM = 8
+LOOK = 0
+DEPTH = 2
+ORDER = (7, 6, 5, 4, 3, 2, 1, 0)
+UNROLL = 4
+MERGE = ((0,), (1, 2), (3, 4), (5, 6), (7,))
 
 
 def ring_offsets(zs):
@@ -60,10 +65,6 @@
             wsem.at[xr],
         )
 
-    for xr in range(XS):
-        for k in range(zs):
-            w_copy(xr, k).start()
-
     gown[...] = gain_ref[...].astype(jnp.float32)
 
     barrier = pltpu.get_barrier_semaphore()
@@ -90,14 +91,18 @@
             for xr in range(1, XS):
                 hello(sec - 1, z_at(offs[k]), x_at(xr))
 
+    for xr in range(XS):
+        for k in range(zs):
+            w_copy(xr, k).start()
+
     greetings = zs - 1 + XS - 1
     greetings = greetings + jnp.where(sec == 0, len(direct) * (XS - 1), 0)
     greetings = greetings + jnp.where(sec < secs - 1, zs + len(direct) * (XS - 1), 0)
     pl.semaphore_wait(barrier, greetings)
 
     def send_block(src, target, b, own):
-        for k in reversed(range(zs)):
-            for xr in range(XS) if k in direct else (0,):
+        for k in ORDER or range(zs):
+            for xr in (2, 1, 3, 0) if k in direct else (0,):
                 sem = zsem.at[b, k] if xr == 0 else xsem.at[b, xr - 1]
                 dst = xbuf.at[b, xr, k]
                 if own and k == 0 and xr == 0:
@@ -109,9 +114,12 @@
                         device_id=dev(target, z_at(-offs[k]), x_at(-xr)), device_id_type=MESH,
                     ).start()
 
-    @pl.when(sec == 0)
-    def _():
-        send_block(prompt_ref.at[pl.ds(0, rows), :], 0, 0, True)
+    ahead = min(DEPTH + 1, nblk)
+
+    @pl.when(sec == 0)
+    def _():
+        for b in range(ahead):
+            send_block(prompt_ref.at[pl.ds(b * rows, rows), :], 0, b, True)
 
     pltpu.make_async_copy(gown, gbuf.at[0, 0], gsem.at[0]).start()
     for k in range(1, zs):
@@ -119,13 +127,6 @@
             src_ref=gown, dst_ref=gbuf.at[0, k], send_sem=ssem.at[3], recv_sem=gsem.at[0],
             device_id=dev(sec, z_at(-offs[k]), x), device_id_type=MESH,
         ).start()
-
-    @pl.when(sec == 0)
-    def _():
-        @pl.loop(1, nblk)
-        def _(b):
-            start = pl.multiple_of(b * rows, rows)
-            send_block(prompt_ref.at[pl.ds(start, rows), :], 0, b, True)
 
     pad = rows
     fpad[...] = jnp.zeros_like(fpad)
@@ -165,24 +166,33 @@
             lo = d * rows - 8 * q + rows - 8
             tbuf[d, :, pl.ds(q * 128, 128)] = gpad[pl.ds(lo, rows), :].astype(jnp.bfloat16)
 
+    for d in range(UNROLL - 1):
+        tbuf[nblk + d] = jnp.zeros(tbuf.shape[1:], jnp.bfloat16)
+        rhs[d] = jnp.zeros(rhs.shape[1:], jnp.bfloat16)
     pbuf[...] = jnp.zeros_like(pbuf)
 
-    pltpu.make_async_copy(gbuf.at[0], gbuf.at[0], gsem.at[0]).wait()
-    for xr in range(1, XS):
-        pltpu.make_async_remote_copy(
-            src_ref=gbuf.at[0], dst_ref=gbuf.at[xr], send_sem=ssem.at[4], recv_sem=gsem.at[xr],
-            device_id=dev(sec, z, x_at(-xr)), device_id_type=MESH,
-        ).start()
-
     def forward(b):
-        for k in fwd:
-            pltpu.make_async_copy(xbuf.at[b, 0, k], xbuf.at[b, 0, k], zsem.at[b, k]).wait()
+        for group in MERGE:
+            group = [k for k in group if k in fwd]
+            if not group:
+                continue
+            for k in group:
+                pltpu.make_async_copy(xbuf.at[b, 0, k], xbuf.at[b, 0, k], zsem.at[b, k]).wait()
+            part = pl.ds(group[0], len(group))
             for xr in (2, 1, 3):
                 pltpu.make_async_remote_copy(
-                    src_ref=xbuf.at[b, 0, k], dst_ref=xbuf.at[b, xr, k],
+                    src_ref=xbuf.at[b, 0, part], dst_ref=xbuf.at[b, xr, part],
                     send_sem=ssem.at[2], recv_sem=xsem.at[b, xr - 1],
                     device_id=dev(sec, z, x_at(-xr)), device_id_type=MESH,
                 ).start()
+
+    def forward_next(b, place):
+        if place == LOOK:
+            then = b + jnp.where(sec == 0, DEPTH, 1)
+
+            @pl.when(then < nblk)
+            def _():
+                forward(then)
 
     def product(b, xr, acc, squares):
         pieces = []
@@ -203,27 +213,60 @@
     lane_group = lax.broadcasted_iota(jnp.int32, (16, 256), 1) // 16
     own_group = lane_group == lax.broadcasted_iota(jnp.int32, (16, 256), 0)
 
+    def spread_gains():
+        pltpu.make_async_copy(gbuf.at[0], gbuf.at[0], gsem.at[0]).wait()
+        for xr in range(1, XS):
+            pltpu.make_async_remote_copy(
+                src_ref=gbuf.at[0], dst_ref=gbuf.at[xr], send_sem=ssem.at[4], recv_sem=gsem.at[xr],
+                device_id=dev(sec, z, x_at(-xr)), device_id_type=MESH,
+            ).start()
+
+    @pl.when(sec > 0)
+    def _():
+        spread_gains()
+
     forward(0)
+
+    @pl.when(sec == 0)
+    def _():
+        spread_gains()
+        for b in range(1, min(DEPTH, nblk)):
+            forward(b)
+
+    @pl.when(sec == 0)
+    def _():
+        @pl.loop(ahead, nblk)
+        def _(b):
+            start = pl.multiple_of(b * rows, rows)
+            send_block(prompt_ref.at[pl.ds(start, rows), :], 0, b, True)
+
     for xr in range(XS):
         pltpu.make_async_copy(wbuf.at[:, xr], wbuf.at[:, xr], wsem.at[xr]).wait()
     for xr in range(1, XS):
         pltpu.make_async_copy(gbuf.at[xr], gbuf.at[xr], gsem.at[xr]).wait()
 
     def block(b, carry):
-        def earlier(d, total):
-            return total + jnp.dot(tbuf[d], rhs[b - d], preferred_element_type=jnp.float32)
-
-        conv = lax.fori_loop(1, b + 1, earlier, jnp.zeros((rows, 256), jnp.float32))
+        def earlier(step, total):
+            for i in range(UNROLL):
+                d = 1 + step * UNROLL + i
+                total = total + jnp.dot(
+                    tbuf[d], rhs[b - d + UNROLL - 1], preferred_element_type=jnp.float32
+                )
+            return total
+
+        conv = lax.fori_loop(
+            0, (b + UNROLL - 1) // UNROLL, earlier, jnp.zeros((rows, 256), jnp.float32)
+        )
         for k in direct:
             pltpu.make_async_copy(xbuf.at[b, 0, k], xbuf.at[b, 0, k], zsem.at[b, k]).wait()
         acc = tuple(jnp.zeros((rows, 256), jnp.float32) for i in range(3))
-        acc, squares = product(b, 0, acc, jnp.zeros((rows, 128), jnp.float32))
-
-        def side(xr, state):
+        state = product(b, 0, acc, jnp.zeros((rows, 128), jnp.float32))
+        forward_next(b, 0)
+        for place, xr in enumerate((1, 3, 2)):
             pltpu.make_async_copy(xbuf.at[b, xr], xbuf.at[b, xr], xsem.at[b, xr - 1]).wait()
-            return product(b, xr, *state)
-
-        acc, squares = lax.fori_loop(1, XS, side, (acc, squares))
+            state = product(b, xr, *state)
+            forward_next(b, place + 1)
+        acc, squares = state
         scale = lax.rsqrt(jnp.sum(squares, axis=1, keepdims=True) / width + EPSILON)
         feats = []
         for i in range(3):
@@ -235,10 +278,10 @@
             )
         kv = feats[1] * feats[2]
         for p in range(rows):
-            rhs[b, pl.ds(p * 16, 16), :] = jnp.where(
+            rhs[b + UNROLL - 1, pl.ds(p * 16, 16), :] = jnp.where(
                 own_group, jnp.broadcast_to(kv[p : p + 1], (16, 256)), 0.0
             ).astype(jnp.bfloat16)
-        conv = conv + jnp.dot(tbuf[0], rhs[b], preferred_element_type=jnp.float32)
+        conv = conv + jnp.dot(tbuf[0], rhs[b + UNROLL - 1], preferred_element_type=jnp.float32)
         start = pl.multiple_of(b * rows, rows)
         result = xbuf[b, 0, 0].astype(jnp.float32) + feats[0] * conv
         o_ref[pl.ds(start, rows), :] = result.astype(jnp.bfloat16)
@@ -250,10 +293,7 @@
         for i in range(3):
             pbuf[i, pl.ds(0, 8), :] = pbuf[i, pl.ds(rows, 8), :]
 
-        @pl.when(b < nblk - 1)
-        def _():
-            forward(b + 1)
-
+        forward_next(b, 4)
         return carry
 
     lax.fori_loop(0, nblk, block, 0)
@@ -302,8 +342,8 @@
                 pltpu.VMEM((3, 8 + rows, 256), jnp.float32),
                 pltpu.VMEM((rows + length, 128), jnp.float32),
                 pltpu.VMEM((rows + length - 8, 128), jnp.float32),
-                pltpu.VMEM((nblk, rows, rows * 16), jnp.bfloat16),
-                pltpu.VMEM((nblk, rows * 16, 256), jnp.bfloat16),
+                pltpu.VMEM((nblk + UNROLL - 1, rows, rows * 16), jnp.bfloat16),
+                pltpu.VMEM((nblk + UNROLL - 1, rows * 16, 256), jnp.bfloat16),
                 pltpu.SemaphoreType.DMA((XS,)),
                 pltpu.SemaphoreType.DMA((nblk, zs)),
                 pltpu.SemaphoreType.DMA((nblk, XS - 1)),

time: 156 us -> 137 us (0.88)
  Pallas kernels: 154 us -> 136 us
    pallas_call x1, Pallas kernels: 154 us -> 136 us  [body(): pl.pallas_call(functools.partial(kernel, (secs, zs, length)), name='relay...]
where the time goes in v2:
time: 137 us
  Pallas kernels  136 us (99%)
  local copies, waits for them, and re-layouts  1.54 us (1%)
    pallas_call x1, Pallas kernels, body(): pl.pallas_call(functools.partial(kernel, (secs, zs, length)), name='relay...  136 us

profile of v2, /device:TPU:25, one launch (start us, length us, event | category | flops | bytes accessed | tf_op | source)
XLA Modules:
  0.0 137.3 jit_solution(4202141049329721256)
XLA Ops:
  0.0 135.7 %relay.1 = bf16[192,256]{1,0:T(8,128)(2,1)} custom-call(bf16[192,256]{1,0:T(8,128)(2,1)} %prompt_ref.1, bf16[1,256]{1,0:T(2,128)(2,1)} %gain_ref.1, bf16[3,8192,256]{2,1,0:T(8,128)(2,1)} %bitcast.10, f32[9,1,256]{2,1,0:T(1,128)} %bitcast.12, f32[16,128]{1,0:T(8,128)} %bitcast.13, f32[16,16]{1,0:T(8,128)} %bitcast.14, f32[16,16]{1,0:T(8,128)} %bitcast.15), custom_call_target="tpu_custom_call" | custom-call | tf_op jit(solution)/shard_map/relay/pallas_call | solution.py:331
  135.7 1.5 %copy.9 = bf16[1,192,256]{2,1,0:T(8,128)(2,1)} copy(bf16[1,192,256]{2,1,0:T(8,128)(2,1)} %bitcast.11) | data formatting | bytes 196608

commit v3 on v2

--- a/solution.py
+++ b/solution.py
@@ -11,10 +11,9 @@
 EPSILON = 1e-06
 BLOCK = 16
 XS = 4
-DIRECT_FROM = 8
 LOOK = 0
 DEPTH = 2
-ORDER = (7, 6, 5, 4, 3, 2, 1, 0)
+ORDER = (0, 7, 6, 5, 4, 3, 2, 1)
 UNROLL = 4
 MERGE = ((0,), (1, 2), (3, 4), (5, 6), (7,))
 
@@ -40,8 +39,6 @@
     nblk = length // rows
     width = zs * XS * 256
     offs = ring_offsets(zs)
-    fwd = [k for k in range(zs) if k < DIRECT_FROM]
-    direct = [k for k in range(zs) if k >= DIRECT_FROM]
     sec = lax.axis_index("section")
     chan = lax.axis_index("chan")
     z = chan // XS
@@ -79,54 +76,54 @@
 
     @pl.when(sec == 0)
     def _():
-        for k in direct:
-            for xr in range(1, XS):
-                hello(sec, z_at(offs[k]), x_at(xr))
+        for k in range(zs):
+            hello(1, z_at(offs[k]), x)
 
     @pl.when(sec > 0)
     def _():
         for k in range(zs):
             hello(sec - 1, z_at(offs[k]), x)
-        for k in direct:
-            for xr in range(1, XS):
-                hello(sec - 1, z_at(offs[k]), x_at(xr))
 
     for xr in range(XS):
         for k in range(zs):
             w_copy(xr, k).start()
 
     greetings = zs - 1 + XS - 1
-    greetings = greetings + jnp.where(sec == 0, len(direct) * (XS - 1), 0)
-    greetings = greetings + jnp.where(sec < secs - 1, zs + len(direct) * (XS - 1), 0)
+    greetings = greetings + jnp.where(sec < secs - 1, zs, 0)
+    greetings = greetings + jnp.where(sec == 1, zs, 0)
     pl.semaphore_wait(barrier, greetings)
 
+    column = [z_at(-offs[k]) * XS + x for k in range(zs)]
+    across = [z * XS + x_at(-xr) for xr in range(XS)]
+
     def send_block(src, target, b, own):
-        for k in ORDER or range(zs):
-            for xr in (2, 1, 3, 0) if k in direct else (0,):
-                sem = zsem.at[b, k] if xr == 0 else xsem.at[b, xr - 1]
-                dst = xbuf.at[b, xr, k]
-                if own and k == 0 and xr == 0:
-                    pltpu.make_async_copy(src, dst, sem).start()
-                else:
-                    pltpu.make_async_remote_copy(
-                        src_ref=src, dst_ref=dst,
-                        send_sem=ssem.at[0 if xr == 0 else 1], recv_sem=sem,
-                        device_id=dev(target, z_at(-offs[k]), x_at(-xr)), device_id_type=MESH,
-                    ).start()
-
-    ahead = min(DEPTH + 1, nblk)
-
-    @pl.when(sec == 0)
-    def _():
-        for b in range(ahead):
-            send_block(prompt_ref.at[pl.ds(b * rows, rows), :], 0, b, True)
+        for k in ORDER:
+            dst, sem = xbuf.at[b, 0, k], zsem.at[b, k]
+            if own and k == 0:
+                pltpu.make_async_copy(src, dst, sem).start()
+            else:
+                pltpu.make_async_remote_copy(
+                    src_ref=src, dst_ref=dst, send_sem=ssem.at[0], recv_sem=sem,
+                    device_id=(target, column[k]), device_id_type=MESH,
+                ).start()
 
     pltpu.make_async_copy(gown, gbuf.at[0, 0], gsem.at[0]).start()
     for k in range(1, zs):
         pltpu.make_async_remote_copy(
-            src_ref=gown, dst_ref=gbuf.at[0, k], send_sem=ssem.at[3], recv_sem=gsem.at[0],
+            src_ref=gown, dst_ref=gbuf.at[0, k], send_sem=ssem.at[2], recv_sem=gsem.at[0],
             device_id=dev(sec, z_at(-offs[k]), x), device_id_type=MESH,
         ).start()
+
+    @pl.when(sec == 0)
+    def _():
+        send_block(prompt_ref.at[pl.ds(0, rows), :], 0, 0, True)
+
+    @pl.when(sec == 1)
+    def _():
+        @pl.loop(1, nblk)
+        def _(b):
+            start = pl.multiple_of(b * rows, rows)
+            send_block(prompt_ref.at[pl.ds(start, rows), :], 0, b, False)
 
     pad = rows
     fpad[...] = jnp.zeros_like(fpad)
@@ -173,17 +170,14 @@
 
     def forward(b):
         for group in MERGE:
-            group = [k for k in group if k in fwd]
-            if not group:
-                continue
             for k in group:
                 pltpu.make_async_copy(xbuf.at[b, 0, k], xbuf.at[b, 0, k], zsem.at[b, k]).wait()
             part = pl.ds(group[0], len(group))
             for xr in (2, 1, 3):
                 pltpu.make_async_remote_copy(
                     src_ref=xbuf.at[b, 0, part], dst_ref=xbuf.at[b, xr, part],
-                    send_sem=ssem.at[2], recv_sem=xsem.at[b, xr - 1],
-                    device_id=dev(sec, z, x_at(-xr)), device_id_type=MESH,
+                    send_sem=ssem.at[1], recv_sem=xsem.at[b, xr - 1],
+                    device_id=(sec, across[xr]), device_id_type=MESH,
                 ).start()
 
     def forward_next(b, place):
@@ -213,32 +207,19 @@
     lane_group = lax.broadcasted_iota(jnp.int32, (16, 256), 1) // 16
     own_group = lane_group == lax.broadcasted_iota(jnp.int32, (16, 256), 0)
 
-    def spread_gains():
-        pltpu.make_async_copy(gbuf.at[0], gbuf.at[0], gsem.at[0]).wait()
-        for xr in range(1, XS):
-            pltpu.make_async_remote_copy(
-                src_ref=gbuf.at[0], dst_ref=gbuf.at[xr], send_sem=ssem.at[4], recv_sem=gsem.at[xr],
-                device_id=dev(sec, z, x_at(-xr)), device_id_type=MESH,
-            ).start()
-
-    @pl.when(sec > 0)
-    def _():
-        spread_gains()
+    pltpu.make_async_copy(gbuf.at[0], gbuf.at[0], gsem.at[0]).wait()
+    for xr in range(1, XS):
+        pltpu.make_async_remote_copy(
+            src_ref=gbuf.at[0], dst_ref=gbuf.at[xr], send_sem=ssem.at[3], recv_sem=gsem.at[xr],
+            device_id=dev(sec, z, x_at(-xr)), device_id_type=MESH,
+        ).start()
 
     forward(0)
 
     @pl.when(sec == 0)
     def _():
-        spread_gains()
         for b in range(1, min(DEPTH, nblk)):
             forward(b)
-
-    @pl.when(sec == 0)
-    def _():
-        @pl.loop(ahead, nblk)
-        def _(b):
-            start = pl.multiple_of(b * rows, rows)
-            send_block(prompt_ref.at[pl.ds(start, rows), :], 0, b, True)
 
     for xr in range(XS):
         pltpu.make_async_copy(wbuf.at[:, xr], wbuf.at[:, xr], wsem.at[xr]).wait()
@@ -257,8 +238,6 @@
         conv = lax.fori_loop(
             0, (b + UNROLL - 1) // UNROLL, earlier, jnp.zeros((rows, 256), jnp.float32)
         )
-        for k in direct:
-            pltpu.make_async_copy(xbuf.at[b, 0, k], xbuf.at[b, 0, k], zsem.at[b, k]).wait()
         acc = tuple(jnp.zeros((rows, 256), jnp.float32) for i in range(3))
         state = product(b, 0, acc, jnp.zeros((rows, 128), jnp.float32))
         forward_next(b, 0)
@@ -303,20 +282,19 @@
 
     @pl.when(sec == 0)
     def _():
-        sent(xbuf.at[:, 0, pl.ds(1, zs - 1)], 0)
-        if direct:
-            sent(xbuf.at[:, pl.ds(1, XS - 1), pl.ds(0, len(direct))], 1)
+        sent(xbuf.at[0, 0, pl.ds(1, zs - 1)], 0)
+
+    @pl.when(sec == 1)
+    def _():
+        sent(xbuf.at[pl.ds(1, nblk - 1), 0], 0)
 
     @pl.when(sec < secs - 1)
     def _():
         sent(xbuf.at[:, 0], 0)
-        if direct:
-            sent(xbuf.at[:, pl.ds(1, XS - 1), pl.ds(0, len(direct))], 1)
-
-    if fwd:
-        sent(xbuf.at[:, pl.ds(1, XS - 1), pl.ds(0, len(fwd))], 2)
-    sent(gbuf.at[0, pl.ds(1, zs - 1)], 3)
-    sent(gbuf.at[pl.ds(1, XS - 1)], 4)
+
+    sent(xbuf.at[:, pl.ds(1, XS - 1)], 1)
+    sent(gbuf.at[0, pl.ds(1, zs - 1)], 2)
+    sent(gbuf.at[pl.ds(1, XS - 1)], 3)
 
 
 def solution(mesh):
@@ -348,7 +326,7 @@
                 pltpu.SemaphoreType.DMA((nblk, zs)),
                 pltpu.SemaphoreType.DMA((nblk, XS - 1)),
                 pltpu.SemaphoreType.DMA((XS,)),
-                pltpu.SemaphoreType.DMA((5,)),
+                pltpu.SemaphoreType.DMA((4,)),
             ],
             compiler_params=pltpu.CompilerParams(
                 collective_id=0, has_side_effects=True, vmem_limit_bytes=56 << 20

time: 137 us -> 135 us (0.985)
  Pallas kernels: 136 us -> 134 us
    pallas_call x1, Pallas kernels: 136 us -> 134 us  [body(): pl.pallas_call(functools.partial(kernel, (secs, zs, length)), name='relay...]
where the time goes in v3:
time: 135 us
  Pallas kernels  134 us (99%)
  local copies, waits for them, and re-layouts  1.54 us (1%)
    pallas_call x1, Pallas kernels, body(): pl.pallas_call(functools.partial(kernel, (secs, zs, length)), name='relay...  134 us

profile of v3, /device:TPU:25, one launch (start us, length us, event | category | flops | bytes accessed | tf_op | source)
XLA Modules:
  0.0 135.3 jit_solution(17579155634779864629)
XLA Ops:
  0.0 133.7 %relay.1 = bf16[192,256]{1,0:T(8,128)(2,1)} custom-call(bf16[192,256]{1,0:T(8,128)(2,1)} %prompt_ref.1, bf16[1,256]{1,0:T(2,128)(2,1)} %gain_ref.1, bf16[3,8192,256]{2,1,0:T(8,128)(2,1)} %bitcast.10, f32[9,1,256]{2,1,0:T(1,128)} %bitcast.12, f32[16,128]{1,0:T(8,128)} %bitcast.13, f32[16,16]{1,0:T(8,128)} %bitcast.14, f32[16,16]{1,0:T(8,128)} %bitcast.15), custom_call_target="tpu_custom_call" | custom-call | tf_op jit(solution)/shard_map/relay/pallas_call | solution.py:309
  133.7 1.5 %copy.9 = bf16[1,192,256]{2,1,0:T(8,128)(2,1)} copy(bf16[1,192,256]{2,1,0:T(8,128)(2,1)} %bitcast.11) | data formatting | bytes 196608

commit v4 on v3

--- a/solution.py
+++ b/solution.py
@@ -9,13 +9,14 @@
 
 MESH = pl.DeviceIdType.MESH
 EPSILON = 1e-06
-BLOCK = 16
+BLOCK = 24
 XS = 4
 LOOK = 0
 DEPTH = 2
 ORDER = (0, 7, 6, 5, 4, 3, 2, 1)
 UNROLL = 4
 MERGE = ((0,), (1, 2), (3, 4), (5, 6), (7,))
+CUTS = ((0, 3), (3, 5), (5, 7), (7, 8))
 
 
 def ring_offsets(zs):
@@ -116,14 +117,13 @@
 
     @pl.when(sec == 0)
     def _():
-        send_block(prompt_ref.at[pl.ds(0, rows), :], 0, 0, True)
+        send_block(prompt_ref.at[0], 0, 0, True)
 
     @pl.when(sec == 1)
     def _():
         @pl.loop(1, nblk)
         def _(b):
-            start = pl.multiple_of(b * rows, rows)
-            send_block(prompt_ref.at[pl.ds(start, rows), :], 0, b, False)
+            send_block(prompt_ref.at[b], 0, b, False)
 
     pad = rows
     fpad[...] = jnp.zeros_like(fpad)
@@ -172,11 +172,12 @@
         for group in MERGE:
             for k in group:
                 pltpu.make_async_copy(xbuf.at[b, 0, k], xbuf.at[b, 0, k], zsem.at[b, k]).wait()
+            cut = [lo <= group[0] < hi for lo, hi in CUTS].index(True)
             part = pl.ds(group[0], len(group))
             for xr in (2, 1, 3):
                 pltpu.make_async_remote_copy(
                     src_ref=xbuf.at[b, 0, part], dst_ref=xbuf.at[b, xr, part],
-                    send_sem=ssem.at[1], recv_sem=xsem.at[b, xr - 1],
+                    send_sem=ssem.at[1], recv_sem=xsem.at[b, xr - 1, cut],
                     device_id=(sec, across[xr]), device_id_type=MESH,
                 ).start()
 
@@ -188,9 +189,9 @@
             def _():
                 forward(then)
 
-    def product(b, xr, acc, squares):
+    def product(b, xr, lo, hi, acc, squares):
         pieces = []
-        for k in range(zs):
+        for k in range(lo, hi):
             piece = xbuf[b, xr, k].astype(jnp.float32)
             square = piece * piece
             squares = squares + (square[:, :128] + square[:, 128:])
@@ -198,7 +199,10 @@
         left = jnp.concatenate(pieces, axis=1)
         return (
             tuple(
-                acc[i] + jnp.dot(left, wbuf[i, xr], preferred_element_type=jnp.float32)
+                acc[i] + jnp.dot(
+                    left, wbuf[i, xr, pl.ds(lo * 256, (hi - lo) * 256), :],
+                    preferred_element_type=jnp.float32,
+                )
                 for i in range(3)
             ),
             squares,
@@ -239,12 +243,13 @@
             0, (b + UNROLL - 1) // UNROLL, earlier, jnp.zeros((rows, 256), jnp.float32)
         )
         acc = tuple(jnp.zeros((rows, 256), jnp.float32) for i in range(3))
-        state = product(b, 0, acc, jnp.zeros((rows, 128), jnp.float32))
+        state = product(b, 0, 0, zs, acc, jnp.zeros((rows, 128), jnp.float32))
         forward_next(b, 0)
-        for place, xr in enumerate((1, 3, 2)):
-            pltpu.make_async_copy(xbuf.at[b, xr], xbuf.at[b, xr], xsem.at[b, xr - 1]).wait()
-            state = product(b, xr, *state)
-            forward_next(b, place + 1)
+        for cut, (lo, hi) in enumerate(CUTS):
+            for xr in (1, 3, 2):
+                part = xbuf.at[b, xr, pl.ds(lo, hi - lo)]
+                pltpu.make_async_copy(part, part, xsem.at[b, xr - 1, cut]).wait()
+                state = product(b, xr, lo, hi, *state)
         acc, squares = state
         scale = lax.rsqrt(jnp.sum(squares, axis=1, keepdims=True) / width + EPSILON)
         feats = []
@@ -261,13 +266,12 @@
                 own_group, jnp.broadcast_to(kv[p : p + 1], (16, 256)), 0.0
             ).astype(jnp.bfloat16)
         conv = conv + jnp.dot(tbuf[0], rhs[b + UNROLL - 1], preferred_element_type=jnp.float32)
-        start = pl.multiple_of(b * rows, rows)
         result = xbuf[b, 0, 0].astype(jnp.float32) + feats[0] * conv
-        o_ref[pl.ds(start, rows), :] = result.astype(jnp.bfloat16)
+        o_ref[b] = result.astype(jnp.bfloat16)
 
         @pl.when(sec < secs - 1)
         def _():
-            send_block(o_ref.at[pl.ds(start, rows), :], sec + 1, b, False)
+            send_block(o_ref.at[b], sec + 1, b, False)
 
         for i in range(3):
             pbuf[i, pl.ds(0, 8), :] = pbuf[i, pl.ds(rows, 8), :]
@@ -309,7 +313,7 @@
         out = pl.pallas_call(
             functools.partial(kernel, (secs, zs, length)),
             name="relay",
-            out_shape=jax.ShapeDtypeStruct((length, local), jnp.bfloat16),
+            out_shape=jax.ShapeDtypeStruct((nblk, rows, local), jnp.bfloat16),
             in_specs=[vmem, vmem, pl.BlockSpec(memory_space=pl.ANY), vmem, vmem, vmem, vmem],
             out_specs=vmem,
             scratch_shapes=[
@@ -324,7 +328,7 @@
                 pltpu.VMEM((nblk + UNROLL - 1, rows * 16, 256), jnp.bfloat16),
                 pltpu.SemaphoreType.DMA((XS,)),
                 pltpu.SemaphoreType.DMA((nblk, zs)),
-                pltpu.SemaphoreType.DMA((nblk, XS - 1)),
+                pltpu.SemaphoreType.DMA((nblk, XS - 1, len(CUTS))),
                 pltpu.SemaphoreType.DMA((XS,)),
                 pltpu.SemaphoreType.DMA((4,)),
             ],
@@ -332,7 +336,7 @@
                 collective_id=0, has_side_effects=True, vmem_limit_bytes=56 << 20
             ),
         )(
-            prompt,
+            prompt.reshape(nblk, rows, local),
             norm_gain,
             in_weight[0].transpose(1, 0, 2),
             feat_taps[0].reshape(9, 1, local),
@@ -340,7 +344,7 @@
             residues[0],
             decay[0],
         )
-        return out[None]
+        return out.reshape(1, length, local)
 
     return jax.shard_map(
         body,

time: 135 us -> 131 us (0.970)
  Pallas kernels: 134 us -> 129 us
    pallas_call x1, Pallas kernels: 134 us -> 129 us  [body(): pl.pallas_call(functools.partial(kernel, (secs, zs, length)), name='relay...]
where the time goes in v4:
time: 131 us; the launch traced here: 130 us
  Pallas kernels  129 us (98%)
  local copies, waits for them, and re-layouts  1.54 us (1%)
    pallas_call x1, Pallas kernels, body(): pl.pallas_call(functools.partial(kernel, (secs, zs, length)), name='relay...  129 us

profile of v4, /device:TPU:25, one launch (start us, length us, event | category | flops | bytes accessed | tf_op | source)
XLA Modules:
  0.0 130.4 jit_solution(9427506795036433506)
XLA Ops:
  0.0 128.9 %relay.1 = bf16[8,24,256]{2,1,0:T(8,128)(2,1)} custom-call(bf16[8,24,256]{2,1,0:T(8,128)(2,1)} %bitcast.13, bf16[1,256]{1,0:T(2,128)(2,1)} %gain_ref.1, bf16[3,8192,256]{2,1,0:T(8,128)(2,1)} %bitcast.11, f32[9,1,256]{2,1,0:T(1,128)} %bitcast.14, f32[16,128]{1,0:T(8,128)} %bitcast.15, f32[16,16]{1,0:T(8,128)} %bitcast.16, f32[16,16]{1,0:T(8,128)} %bitcast.17), custom_call_target="tpu_custom_call" | custom-call | tf_op jit(solution)/shard_map/relay/pallas_call | solution.py:313
  128.9 1.5 %copy.9 = bf16[1,192,256]{2,1,0:T(8,128)(2,1)} copy(bf16[1,192,256]{2,1,0:T(8,128)(2,1)} %bitcast.12) | data formatting | bytes 196608

commit v5 on v4

--- a/solution.py
+++ b/solution.py
@@ -12,7 +12,7 @@
 BLOCK = 24
 XS = 4
 LOOK = 0
-DEPTH = 2
+DEPTH = 3
 ORDER = (0, 7, 6, 5, 4, 3, 2, 1)
 UNROLL = 4
 MERGE = ((0,), (1, 2), (3, 4), (5, 6), (7,))
@@ -174,7 +174,7 @@
                 pltpu.make_async_copy(xbuf.at[b, 0, k], xbuf.at[b, 0, k], zsem.at[b, k]).wait()
             cut = [lo <= group[0] < hi for lo, hi in CUTS].index(True)
             part = pl.ds(group[0], len(group))
-            for xr in (2, 1, 3):
+            for xr in (1, 3, 2):
                 pltpu.make_async_remote_copy(
                     src_ref=xbuf.at[b, 0, part], dst_ref=xbuf.at[b, xr, part],
                     send_sem=ssem.at[1], recv_sem=xsem.at[b, xr - 1, cut],

time: 131 us -> 130 us (level)
  no operation moved by 1% of the time
where the time goes in v5:
time: 130 us
  Pallas kernels  128 us (98%)
  local copies, waits for them, and re-layouts  1.54 us (1%)
    pallas_call x1, Pallas kernels, body(): pl.pallas_call(functools.partial(kernel, (secs, zs, length)), name='relay...  128 us

profile of v5, /device:TPU:25, one launch (start us, length us, event | category | flops | bytes accessed | tf_op | source)
XLA Modules:
  0.0 130.0 jit_solution(3711944895016655480)
XLA Ops:
  0.0 128.5 %relay.1 = bf16[8,24,256]{2,1,0:T(8,128)(2,1)} custom-call(bf16[8,24,256]{2,1,0:T(8,128)(2,1)} %bitcast.13, bf16[1,256]{1,0:T(2,128)(2,1)} %gain_ref.1, bf16[3,8192,256]{2,1,0:T(8,128)(2,1)} %bitcast.11, f32[9,1,256]{2,1,0:T(1,128)} %bitcast.14, f32[16,128]{1,0:T(8,128)} %bitcast.15, f32[16,16]{1,0:T(8,128)} %bitcast.16, f32[16,16]{1,0:T(8,128)} %bitcast.17), custom_call_target="tpu_custom_call" | custom-call | tf_op jit(solution)/shard_map/relay/pallas_call | solution.py:313
  128.5 1.5 %copy.9 = bf16[1,192,256]{2,1,0:T(8,128)(2,1)} copy(bf16[1,192,256]{2,1,0:T(8,128)(2,1)} %bitcast.12) | data formatting | bytes 196608
